TPU v7x, 32 devices: a whole 2x2x4 slice. The times are simulated.
32 devices in a mesh: grid: 1, samp: 32 (over z, y, x, core).
Axes of the slice: x: 2, y: 2, z: 4, core: 2. Of those that a mesh axis runs over, the one named last changes fastest.
Arguments:
- summary: bfloat16 [65536, 1024], P('samp'), may hold values from -10 to 10
- kernel: bfloat16 [1024, 4096], P(None, 'grid'), may hold values from -1 to 1
- grid_offset: float32 [4096], P('grid'), may hold values from -130 to 130
- log_prior: float32 [65536], P('samp'), may hold values from -6 to 6
- tile_event: int32 [512], P('samp'), may hold values from 0 to 63, as said below
- tile_live: int32 [512], P('samp'), may hold values from 2 to 128
Outputs:
- log_evidence: float32 [64, 4096], P('samp', 'grid')
- ess_fraction: float32 [64, 4096], P('samp', 'grid')
- log_posterior: float32 [4096], P('grid')
Inputs may be any that keep to these rules, and one draw needn't show every extreme that they name: `tile_event`: every event owns at least one tile.
All inputs are finite; a program needn't handle non-finite values.
Results may differ from a plain program's by a relative error of at most 0.0003.
Values sent between devices are 32-bit elements; how exact they have to be, the bound alone decides.
No kernel may reach another device: no remote copies, remote signals or barrier semaphores. Data moves between devices by JAX's collectives and lax.ppermute only.
A program may use at most 128 MiB of HBM per device.

v0:
```python
import jax
import jax.numpy as jnp
from jax import lax
from jax.sharding import PartitionSpec as P

EVENTS = 64


def body(summary, kernel, grid_offset, log_prior, tile_event, tile_live):
    row_count = summary.shape[0]
    grid_cols = kernel.shape[1]
    tile_count = tile_event.shape[0]
    tile_rows = row_count // tile_count
    scores = jnp.dot(summary, kernel, preferred_element_type=jnp.float32)
    scores = scores + grid_offset[None, :] - log_prior[:, None]
    scores = scores.reshape(tile_count, tile_rows, grid_cols)
    is_live = lax.broadcasted_iota(jnp.int32, (tile_count, tile_rows), 1) < tile_live[:, None]
    masked = jnp.where(is_live[:, :, None], scores, jnp.float32(-1e30))
    tile_max = jnp.max(masked, axis=1)
    shifted = jnp.exp(masked - tile_max[:, None, :])
    tile_first = jnp.sum(shifted, axis=1)
    tile_second = jnp.sum(shifted * shifted, axis=1)
    member = tile_event[None, :] == lax.broadcasted_iota(jnp.int32, (EVENTS, tile_count), 0)
    local_peak = jnp.max(
        jnp.where(member[:, :, None], tile_max[None, :, :], jnp.float32(-1e30)), axis=1
    )
    live_count = jnp.sum(jnp.where(member, tile_live[None, :], 0), axis=1).astype(jnp.float32)
    factor = jnp.exp(tile_max - local_peak[tile_event])
    member_float = member.astype(jnp.float32)
    local_first = jnp.dot(member_float, tile_first * factor, precision=lax.Precision.HIGHEST)
    local_second = jnp.dot(
        member_float, tile_second * factor * factor, precision=lax.Precision.HIGHEST
    )
    got_peak, got_first, got_second, got_count = (
        lax.all_to_all(local_peak[:, None, :], "samp", split_axis=0, concat_axis=1, tiled=True),
        lax.all_to_all(local_first[:, None, :], "samp", split_axis=0, concat_axis=1, tiled=True),
        lax.all_to_all(local_second[:, None, :], "samp", split_axis=0, concat_axis=1, tiled=True),
        lax.all_to_all(live_count[:, None, None], "samp", split_axis=0, concat_axis=1, tiled=True),
    )
    event_peak = jnp.max(got_peak, axis=1)
    rescale = jnp.exp(got_peak - event_peak[:, None, :])
    first_sum = jnp.sum(got_first * rescale, axis=1)
    second_sum = jnp.sum(got_second * rescale * rescale, axis=1)
    total_live = jnp.sum(got_count[:, :, 0], axis=1)
    log_evidence = event_peak + jnp.log(first_sum) - jnp.log(total_live)[:, None]
    ess_fraction = first_sum * first_sum / (second_sum * total_live[:, None])
    loglik = lax.psum(jnp.sum(log_evidence, axis=0), "samp") / jnp.float32(EVENTS)
    local_top = jnp.max(loglik)
    grid_top = lax.pmax(local_top, "grid")
    grid_mass = lax.psum(jnp.sum(jnp.exp(loglik - grid_top)), "grid")
    log_posterior = loglik - (grid_top + jnp.log(grid_mass))
    return (log_evidence, ess_fraction, log_posterior)


def solution(mesh):
    in_specs = (P("samp", None), P(None, "grid"), P("grid"), P("samp"), P("samp"), P("samp"))
    out_specs = (P("samp", "grid"), P("samp", "grid"), P("grid"))
    return jax.shard_map(body, mesh=mesh, in_specs=in_specs, out_specs=out_specs, check_vma=False)
```

profile of v0, /device:TPU:0, one launch (start us, length us, event | category | flops | bytes accessed | tf_op | source)
XLA Modules:
  0.0 201.7 jit_solution(212108620532806428)
XLA Ops:
  0.6 0.0 copy-start
  0.6 0.0 copy-start.1
  0.7 0.8 select_reduce_fusion.2
  1.4 0.7 copy.19
  2.1 7.3 %all-to-all-start.2 = ((f32[64,1,1]{2,1,0:T(1,128)}), f32[64,1,1]{2,1,0:T(1,128)S(1)}, u32[]{:S(2)}, u32[]{:S(2)}) async-start(f32[64,1,1]{2,1,0:T(1,128)} %copy.19), calls=%async_computation.2 | async-start | bytes 65536 | tf_op jit(solution)/shard_map/all_to_all | solution.py:38
  9.5 0.7 iota_compare_fusion
  10.2 0.7 iota_compare_fusion.1
  10.9 0.7 compare_select_fusion
  11.6 0.1 copy.15
  11.7 25.7 %select_reduce_fusion = (f32[16,4096]{1,0:T(8,128)S(1)}, f32[2048,4096]{1,0:T(8,128)}) fusion(f32[2048]{0:T(1024)} %param.9, f32[4096]{0:T(1024)} %param.8, pred[16,128]{1,0:T(8,128)(4,1)S(1)} %iota_compare_fusion, bf16[2048,1024]{1,0:T(8,128)(2,1)} %param.6, bf16[1024,4096]{1,0:T(8,128)(2,1)} %param.7), kind=kOutput, calls=%fused_computation.4 | convolution fusion | flops 17213358080 | bytes 46426112 | tf_op jit(solution)/shard_map/dot_general | solution.py:14
  37.4 0.0 copy-start.2
  37.4 0.0 copy-done
  37.4 0.0 copy-done.1
  37.4 17.1 %multiply_reduce_fusion = (f32[16,4096]{1,0:T(8,128)S(1)}, f32[16,4096]{1,0:T(8,128)S(1)}) fusion(f32[2048,4096]{1,0:T(8,128)} %get-tuple-element.11, f32[16,4096]{1,0:T(8,128)S(1)} %get-tuple-element.10, f32[2048]{0:T(1024)S(1)} %copy-done.1, f32[4096]{0:T(1024)S(1)} %copy-done, pred[16,128]{1,0:T(8,128)(4,1)S(1)} %iota_compare_fusion), kind=kLoop, calls=%fused_computation.1 | loop fusion | flops 58589184 | bytes 34367488 | tf_op jit(solution)/shard_map/reduce_sum | solution.py:22
  54.6 5.5 %select_reduce_fusion.1 = f32[64,4096]{1,0:T(8,128)S(1)} fusion(f32[16,4096]{1,0:T(8,128)S(1)} %get-tuple-element.10, pred[64,16]{1,0:T(8,128)(4,1)S(1)} %copy.15), kind=kLoop, calls=%fused_computation.6 | loop fusion | flops 8126464 | bytes 1311744 | tf_op jit(solution)/shard_map/reduce_max | solution.py:24
  60.1 0.6 gather_fusion
  60.8 0.0 copy-done.2
  60.8 0.7 convolution_bitcast_fusion.1
  61.5 2.1 %copy.17 = f32[64,1,4096]{2,1,0:T(1,128)} copy(f32[64,1,4096]{2,0,1:T(8,128)S(1)} %convolution_bitcast_fusion.1) | data formatting | bytes 2097152 | tf_op jit(solution)/shard_map/broadcast_in_dim | solution.py:36
  63.6 0.0 all-to-all-done.2
  63.6 5.8 %all-to-all-start.1 = ((f32[64,1,4096]{2,1,0:T(1,128)}), f32[64,1,4096]{2,1,0:T(1,128)S(1)}, u32[]{:S(2)}, u32[]{:S(2)}) async-start(f32[64,1,4096]{2,1,0:T(1,128)} %copy.17), calls=%async_computation.1 | async-start | bytes 2097152 | tf_op jit(solution)/shard_map/all_to_all | solution.py:36
  69.4 2.1 %copy.16 = f32[64,1,4096]{2,1,0:T(1,128)} copy(f32[64,1,4096]{2,0,1:T(8,128)S(1)} %bitcast.39) | data formatting | bytes 2097152 | tf_op jit(solution)/shard_map/broadcast_in_dim | solution.py:35
  71.5 24.1 %all-to-all-done.1 = f32[64,1,4096]{2,1,0:T(1,128)S(1)} async-done(((f32[64,1,4096]{2,1,0:T(1,128)}), f32[64,1,4096]{2,1,0:T(1,128)S(1)}, u32[]{:S(2)}, u32[]{:S(2)}) %all-to-all-start.1) | async-done | bytes 1048608 | tf_op jit(solution)/shard_map/all_to_all | solution.py:36
  95.6 3.6 %all-to-all-start = ((f32[64,1,4096]{2,1,0:T(1,128)}), f32[64,1,4096]{2,1,0:T(1,128)S(1)}, u32[]{:S(2)}, u32[]{:S(2)}) async-start(f32[64,1,4096]{2,1,0:T(1,128)} %copy.16), calls=%async_computation | async-start | bytes 2097152 | tf_op jit(solution)/shard_map/all_to_all | solution.py:35
  99.3 0.7 convolution_bitcast_fusion
  100.0 2.1 %copy.20 = f32[64,1,4096]{2,1,0:T(1,128)} copy(f32[64,1,4096]{2,0,1:T(8,128)S(1)} %convolution_bitcast_fusion) | data formatting | bytes 2097152 | tf_op jit(solution)/shard_map/broadcast_in_dim | solution.py:37
  102.1 23.4 %all-to-all-done = f32[64,1,4096]{2,1,0:T(1,128)S(1)} async-done(((f32[64,1,4096]{2,1,0:T(1,128)}), f32[64,1,4096]{2,1,0:T(1,128)S(1)}, u32[]{:S(2)}, u32[]{:S(2)}) %all-to-all-start) | async-done | bytes 1048608 | tf_op jit(solution)/shard_map/all_to_all | solution.py:35
  125.5 3.8 %all-to-all-start.3 = ((f32[64,1,4096]{2,1,0:T(1,128)}), f32[64,1,4096]{2,1,0:T(1,128)S(1)}, u32[]{:S(2)}, u32[]{:S(2)}) async-start(f32[64,1,4096]{2,1,0:T(1,128)} %copy.20), calls=%async_computation.3 | async-start | bytes 2097152 | tf_op jit(solution)/shard_map/all_to_all | solution.py:37
  129.3 0.6 reduce.4
  129.9 0.1 all_to_all.57
  130.0 0.9 reduce_max.38
  131.0 24.3 %all-to-all-done.3 = f32[64,1,4096]{2,1,0:T(1,128)S(1)} async-done(((f32[64,1,4096]{2,1,0:T(1,128)}), f32[64,1,4096]{2,1,0:T(1,128)S(1)}, u32[]{:S(2)}, u32[]{:S(2)}) %all-to-all-start.3) | async-done | bytes 1048608 | tf_op jit(solution)/shard_map/all_to_all | solution.py:37
  155.3 3.2 %fusion.1 = (f32[2,4096]{1,0:T(2,128)S(1)}, f32[2,4096]{1,0:T(2,128)S(1)}) fusion(f32[32,2,1,4096]{3,2,1,0:T(1,128)S(1)} %bitcast.43, f32[2,4096]{1,0:T(2,128)S(1)} %reduce_max.38, f32[2,32,1,4096]{3,2,0,1:T(1,128)S(1)} %bitcast.41, f32[32,2,1,4096]{3,2,1,0:T(1,128)S(1)} %bitcast.42), kind=kLoop, calls=%fused_computation.10 | loop fusion | flops 1556480 | bytes 3244032 | tf_op jit(solution)/shard_map/reduce_sum | solution.py:43
  158.5 0.7 fusion.7
  159.2 38.6 %psum.6 = f32[4096]{0:T(1024)S(1)} all-reduce(f32[4096]{0:T(1024)S(1)} %get-tuple-element.7), channel_id=1, replica_groups=mesh['grid'=1,'samp'=32] {'samp'}, use_global_device_ids=true, to_apply=%region_10.11 | all-reduce | flops 4096 | bytes 32768 | tf_op jit(solution)/shard_map/psum | solution.py:47
  197.8 0.6 multiply_reduce_fusion.1
  198.4 1.3 exponential_reduce_fusion
  201.1 0.6 multiply_subtract_fusion
  (4 shorter events, 0.0 us)
Async XLA Ops:
  0.6 36.8 %copy-start = (f32[4096]{0:T(1024)S(1)}, f32[4096]{0:T(1024)}, u32[]{:S(2)}) copy-start(f32[4096]{0:T(1024)} %param.8) | copy-start | bytes 49156
  0.6 36.8 %copy-start.1 = (f32[2048]{0:T(1024)S(1)}, f32[2048]{0:T(1024)}, u32[]{:S(2)}) copy-start(f32[2048]{0:T(1024)} %param.9) | copy-start | bytes 24580
  2.1 61.5 %all-to-all-start.2 = ((f32[64,1,1]{2,1,0:T(1,128)}), f32[64,1,1]{2,1,0:T(1,128)S(1)}, u32[]{:S(2)}, u32[]{:S(2)}) async-start(f32[64,1,1]{2,1,0:T(1,128)} %copy.19), calls=%async_computation.2 | async-start | bytes 65536 | tf_op jit(solution)/shard_map/all_to_all | solution.py:38
  37.4 23.3 %copy-start.2 = (s32[16]{0:T(128)S(1)}, s32[16]{0:T(128)}, u32[]{:S(2)}) copy-start(s32[16]{0:T(128)} %param.10) | copy-start | bytes 196
  63.6 32.0 %all-to-all-start.1 = ((f32[64,1,4096]{2,1,0:T(1,128)}), f32[64,1,4096]{2,1,0:T(1,128)S(1)}, u32[]{:S(2)}, u32[]{:S(2)}) async-start(f32[64,1,4096]{2,1,0:T(1,128)} %copy.17), calls=%async_computation.1 | async-start | bytes 2097152 | tf_op jit(solution)/shard_map/all_to_all | solution.py:36
  95.6 29.8 %all-to-all-start = ((f32[64,1,4096]{2,1,0:T(1,128)}), f32[64,1,4096]{2,1,0:T(1,128)S(1)}, u32[]{:S(2)}, u32[]{:S(2)}) async-start(f32[64,1,4096]{2,1,0:T(1,128)} %copy.16), calls=%async_computation | async-start | bytes 2097152 | tf_op jit(solution)/shard_map/all_to_all | solution.py:35
  125.5 29.8 %all-to-all-start.3 = ((f32[64,1,4096]{2,1,0:T(1,128)}), f32[64,1,4096]{2,1,0:T(1,128)S(1)}, u32[]{:S(2)}, u32[]{:S(2)}) async-start(f32[64,1,4096]{2,1,0:T(1,128)} %copy.20), calls=%async_computation.3 | async-start | bytes 2097152 | tf_op jit(solution)/shard_map/all_to_all | solution.py:37
where the time goes:
time: 202 us
  waiting for transfers between devices  71.9 us (36%)
  blocking collectives  38.6 us (19%)
  other arithmetic  33.5 us (17%)
  matrix products  27.1 us (13%)
  starting transfers between devices  20.6 us (10%)
  local copies, waits for them, and re-layouts  7.87 us (4%)
  between operations  2.16 us (1%)
    psum x1, blocking collectives, body(): lax.psum(jnp.sum(log_evidence, axis=0), 'samp') / jnp.float32(EVENTS)  38.6 us
    dot_general x1, matrix products, body(): scores = jnp.dot(summary, kernel, preferred_element_type=jnp.float32)  25.7 us
    all_to_all x1, waiting for transfers between devices, body(): lax.all_to_all(local_second[:, None, :], 'samp', split_axis=0, concat_axi...  24.3 us
    all_to_all x1, waiting for transfers between devices, body(): lax.all_to_all(local_first[:, None, :], 'samp', split_axis=0, concat_axis...  24.1 us
    all_to_all x1, waiting for transfers between devices, body(): lax.all_to_all(local_peak[:, None, :], 'samp', split_axis=0, concat_axis=...  23.4 us
    reduce_sum x1, other arithmetic, body(): tile_second = jnp.sum(shifted * shifted, axis=1)  17.1 us
    all_to_all x1, starting transfers between devices, body(): lax.all_to_all(live_count[:, None, None], 'samp', split_axis=0, concat_ax...  7.33 us
    all_to_all x1, starting transfers between devices, body(): lax.all_to_all(local_first[:, None, :], 'samp', split_axis=0, concat_axis...  5.83 us
  transfers between devices with their start and end apart: 4, of which 3 were waited for; matrix products, arithmetic and copies ran while one was open for 30% of the time, Pallas kernels for 0%

commit v1 on v0

--- a/solution.py
+++ b/solution.py
@@ -1,12 +1,334 @@
+import functools
+
 import jax
 import jax.numpy as jnp
 from jax import lax
+from jax.experimental import pallas as pl
+from jax.experimental.pallas import tpu as pltpu
 from jax.sharding import PartitionSpec as P
 
 EVENTS = 64
-
-
-def body(summary, kernel, grid_offset, log_prior, tile_event, tile_live):
+LANES = 128
+GROUP = 16
+CHUNK = 256
+BLOCK = 512
+NEG = -1e30
+DEAD = 1e30
+
+
+def stats_kernel(
+    tiles, tile_rows, depth, cols, event_ref, live_ref, offset_ref, prior_ref, summary_ref, kernel_ref,
+    out_ref, lhs, rhs, prior, score_a, score_b, top, peak, first, second, owner, start, row_sem, col_sem,
+):
+    blocks = cols // BLOCK
+    per_tile = tile_rows // GROUP
+    sizes = [1 << k for k in reversed(range(per_tile.bit_length()))]
+    stride = 2 * tiles + 1
+
+    def row_copies(act):
+        for t in range(tiles):
+            count = lax.div(live_ref[t] + (GROUP - 1), GROUP)
+            base = start[t]
+            for k, size in enumerate(sizes):
+                done = lax.bitwise_and(count, ~(2 * size - 1))
+
+                @pl.when(lax.bitwise_and(count, size) != 0)
+                def _():
+                    copy = pltpu.make_async_copy(
+                        summary_ref.at[pl.ds(pl.multiple_of(t * tile_rows + done * GROUP, GROUP), size * GROUP)],
+                        lhs.at[pl.ds(pl.multiple_of((base + done) * GROUP, GROUP), size * GROUP)],
+                        row_sem.at[t, k],
+                    )
+                    act(copy)
+
+    def col_copy(n):
+        return pltpu.make_async_copy(kernel_ref.at[:, pl.ds(n * BLOCK, BLOCK)], rhs.at[n], col_sem.at[n])
+
+    total = jnp.int32(0)
+    for t in range(tiles):
+        start[t] = total
+        total = total + lax.div(live_ref[t] + (GROUP - 1), GROUP)
+    row_copies(lambda copy: copy.start())
+    for n in range(blocks):
+        col_copy(n).start()
+
+    chunk_groups = CHUNK // GROUP
+    chunks = lax.div(total + (chunk_groups - 1), chunk_groups)
+    for t in range(tiles):
+        count = lax.div(live_ref[t] + (GROUP - 1), GROUP)
+
+        def mark(j, carry):
+            owner[start[t] + j] = t
+            return carry
+
+        lax.fori_loop(0, count, mark, 0)
+        row_at = lax.broadcasted_iota(jnp.int32, (1, tile_rows), 1)
+        held = jnp.where(row_at < live_ref[t], prior_ref[t : t + 1, :], jnp.float32(DEAD))
+        spread = jnp.broadcast_to(held, (LANES, tile_rows)).T
+        prior[pl.ds(pl.multiple_of(start[t] * GROUP, GROUP), tile_rows), :] = spread
+    for j in range(chunk_groups):
+        owner[total + j] = tiles
+
+    top[...] = jnp.full(top.shape, NEG, jnp.float32)
+    first[...] = jnp.zeros(first.shape, jnp.float32)
+    second[...] = jnp.zeros(second.shape, jnp.float32)
+    peak[...] = jnp.zeros(peak.shape, jnp.float32)
+    row_copies(lambda copy: copy.wait())
+
+    def slot_of(tile, w):
+        return pl.ds(pl.multiple_of(tile * 8 + w * (8 * tiles + 8), 8), 8)
+
+    def products(n, c, score):
+        row = pl.multiple_of(c * CHUNK, CHUNK)
+        rows = lhs[pl.ds(row, CHUNK), :]
+        for h in range(BLOCK // 256):
+            part = jnp.dot(rows, rhs[n, :, h * 256 : (h + 1) * 256], preferred_element_type=jnp.float32)
+            for g in range(chunk_groups):
+                at = pl.ds(pl.multiple_of(row + g * GROUP, GROUP), GROUP)
+                held = prior[at, :]
+                for w in range(256 // LANES):
+                    lane = pl.ds(h * 256 + w * LANES, LANES)
+                    slot = slot_of(owner[c * chunk_groups + g], h * 2 + w)
+                    value = part[g * GROUP : (g + 1) * GROUP, w * LANES : (w + 1) * LANES] - held
+                    score[at, lane] = value
+                    top[slot, :] = jnp.maximum(top[slot, :], jnp.maximum(value[:8], value[8:]))
+
+    def sums(c, score):
+        row = pl.multiple_of(c * CHUNK, CHUNK)
+        for g in range(chunk_groups):
+            at = pl.ds(pl.multiple_of(row + g * GROUP, GROUP), GROUP)
+            tile = owner[c * chunk_groups + g]
+            for w in range(BLOCK // LANES):
+                slot = slot_of(tile, w)
+                level = peak[pl.ds(tile + w * (tiles + 8), 8, stride=0), :]
+                value = score[at, pl.ds(w * LANES, LANES)]
+                low, high = jnp.exp(value[:8] - level), jnp.exp(value[8:] - level)
+                first[slot, :] = first[slot, :] + (low + high)
+                second[slot, :] = second[slot, :] + (low * low + high * high)
+
+    def fold(ref, half, w, join):
+        parts = [ref[pl.ds(w * (8 * tiles + 8) + half * 64 + i, 8, stride=8), :] for i in range(8)]
+        while len(parts) > 1:
+            parts = [join(a, b) for a, b in zip(parts[::2], parts[1::2])]
+        return parts[0]
+
+    def close_top():
+        for half in range(tiles // 8):
+            for w in range(BLOCK // LANES):
+                peak[pl.ds(w * (tiles + 8) + half * 8, 8), :] = fold(top, half, w, jnp.maximum)
+        top[...] = jnp.full(top.shape, NEG, jnp.float32)
+
+    def close_sums(n):
+        for half in range(tiles // 8):
+            for w in range(BLOCK // LANES):
+                one = fold(first, half, w, jnp.add)
+                two = fold(second, half, w, jnp.add)
+                level = peak[pl.ds(w * (tiles + 8) + half * 8, 8), :]
+                shift = offset_ref[:, pl.ds(pl.multiple_of(n * BLOCK + w * LANES, LANES), LANES)]
+                base = (n * (BLOCK // LANES) + w) * stride + half * 8
+                out_ref[pl.ds(base, 8), :] = level + jnp.log(one) + shift
+                out_ref[pl.ds(base + tiles, 8), :] = two / (one * one)
+        first[...] = jnp.zeros(first.shape, jnp.float32)
+        second[...] = jnp.zeros(second.shape, jnp.float32)
+
+    def each_chunk(work):
+        def step(c, carry):
+            work(c)
+            return carry
+
+        lax.fori_loop(0, chunks, step, 0)
+
+    col_copy(0).wait()
+    each_chunk(lambda c: products(0, c, score_a))
+
+    def step(n, now, before):
+        close_top()
+        col_copy(n).wait()
+
+        def work(c):
+            products(n, c, now)
+            sums(c, before)
+
+        each_chunk(work)
+        close_sums(n - 1)
+
+    def pair(i, carry):
+        step(2 * i + 1, score_b, score_a)
+
+        @pl.when(i < blocks // 2 - 1)
+        def _():
+            step(2 * i + 2, score_a, score_b)
+
+        return carry
+
+    lax.fori_loop(0, blocks // 2, pair, 0)
+    close_top()
+    each_chunk(lambda c: sums(c, score_b))
+    close_sums(blocks - 1)
+
+    lane_at = lax.broadcasted_iota(jnp.int32, (1, LANES), 1)
+    facts = jnp.zeros((1, LANES), jnp.float32)
+    for t in range(tiles):
+        facts = jnp.where(lane_at == t, event_ref[t].astype(jnp.float32), facts)
+        facts = jnp.where(lane_at == tiles + t, live_ref[t].astype(jnp.float32), facts)
+    for d in range(cols // LANES):
+        out_ref[d * stride + 2 * tiles : d * stride + 2 * tiles + 1, :] = facts
+
+
+def tile_stats(summary, kernel, grid_offset, log_prior, tile_event, tile_live):
+    rows, depth = summary.shape
+    cols = kernel.shape[1]
+    tiles = tile_event.shape[0]
+    tile_rows = rows // tiles
+    stride = 2 * tiles + 1
+    smem = pl.BlockSpec(memory_space=pltpu.SMEM)
+    vmem = pl.BlockSpec(memory_space=pltpu.VMEM)
+    hbm = pl.BlockSpec(memory_space=pl.ANY)
+    f32 = jnp.float32
+    return pl.pallas_call(
+        functools.partial(stats_kernel, tiles, tile_rows, depth, cols),
+        out_shape=jax.ShapeDtypeStruct((cols // LANES * stride, LANES), f32),
+        in_specs=[smem, smem, vmem, vmem, hbm, hbm],
+        out_specs=vmem,
+        scratch_shapes=[
+            pltpu.VMEM((rows + CHUNK, depth), jnp.bfloat16),
+            pltpu.VMEM((cols // BLOCK, depth, BLOCK), jnp.bfloat16),
+            pltpu.VMEM((rows + CHUNK, LANES), f32),
+            pltpu.VMEM((rows + CHUNK, BLOCK), f32),
+            pltpu.VMEM((rows + CHUNK, BLOCK), f32),
+            pltpu.VMEM((BLOCK // LANES * (8 * tiles + 8), LANES), f32),
+            pltpu.VMEM((BLOCK // LANES * (tiles + 8), LANES), f32),
+            pltpu.VMEM((BLOCK // LANES * (8 * tiles + 8), LANES), f32),
+            pltpu.VMEM((BLOCK // LANES * (8 * tiles + 8), LANES), f32),
+            pltpu.SMEM((rows // GROUP + CHUNK // GROUP,), jnp.int32),
+            pltpu.SMEM((tiles,), jnp.int32),
+            pltpu.SemaphoreType.DMA((tiles, (tile_rows // GROUP).bit_length())),
+            pltpu.SemaphoreType.DMA((cols // BLOCK,)),
+        ],
+        compiler_params=pltpu.CompilerParams(vmem_limit_bytes=48 << 20),
+    )(
+        tile_event, tile_live, grid_offset.reshape(1, cols), log_prior.reshape(tiles, tile_rows), summary, kernel,
+    )
+
+
+def split3(x):
+    high = x.astype(jnp.bfloat16)
+    rest = x - high.astype(jnp.float32)
+    middle = rest.astype(jnp.bfloat16)
+    low = (rest - middle.astype(jnp.float32)).astype(jnp.bfloat16)
+    return high, middle, low
+
+
+def merge_kernel(devices, tiles, got_ref, out_ref, level, event, ratio, live, peak_of, peak, kept):
+    stride = 2 * tiles + 1
+    total = devices * tiles
+    facts = got_ref[pl.ds(2 * tiles, devices, stride=stride), :]
+    for i in range(tiles):
+        at = slice(i * devices, (i + 1) * devices)
+        level[at, :] = got_ref[pl.ds(i, devices, stride=stride), :]
+        ratio[at, :] = got_ref[pl.ds(tiles + i, devices, stride=stride), :]
+        event[at, :] = jnp.broadcast_to(facts[:, i : i + 1], (devices, LANES))
+        live[at, :] = jnp.broadcast_to(facts[:, tiles + i : tiles + i + 1], (devices, LANES))
+
+    def find(e, carry):
+        name = e.astype(jnp.float32)
+        parts = [jnp.full((8, LANES), NEG, jnp.float32) for _ in range(4)]
+        for v in range(total // 8):
+            at = slice(v * 8, v * 8 + 8)
+            parts[v % 4] = jnp.maximum(
+                parts[v % 4], jnp.where(event[at, :] == name, level[at, :], jnp.float32(NEG))
+            )
+        best = jnp.maximum(jnp.maximum(parts[0], parts[1]), jnp.maximum(parts[2], parts[3]))
+        best = jnp.max(best, axis=0, keepdims=True)
+        peak[pl.ds(e, 1), :] = best
+        wide = jnp.broadcast_to(best, (8, LANES))
+        for v in range(total // 8):
+            at = slice(v * 8, v * 8 + 8)
+            peak_of[at, :] = jnp.where(event[at, :] == name, wide, peak_of[at, :])
+        return carry
+
+    lax.fori_loop(0, EVENTS, find, 0)
+    one = jnp.exp(level[...] - peak_of[...])
+    two = ratio[...] * one * one
+    lanes = lax.broadcasted_iota(jnp.int32, (total, LANES), 1).astype(jnp.float32)
+    chosen = jnp.where(event[...] == lanes, jnp.float32(1), jnp.float32(0)).astype(jnp.bfloat16)
+    right = jnp.concatenate(split3(one) + split3(two) + (live[...].astype(jnp.bfloat16),), axis=1)
+    sums = lax.dot_general(chosen, right, (((0,), (0,)), ((), ())), preferred_element_type=jnp.float32)
+    part = [sums[:EVENTS, k * LANES : (k + 1) * LANES] for k in range(7)]
+    first = part[0] + part[1] + part[2]
+    second = part[3] + part[4] + part[5]
+    count = part[6]
+    evidence = peak[...] + jnp.log(first) - jnp.log(count)
+    kept[:EVENTS, :] = evidence
+    kept[EVENTS:, :] = first * first / (second * count)
+    own = EVENTS // devices
+    out_stride = 2 * own + 1
+    for k in range(own):
+        out_ref[pl.ds(k, devices, stride=out_stride), :] = kept[pl.ds(k, devices, stride=own), :]
+        out_ref[pl.ds(own + k, devices, stride=out_stride), :] = kept[pl.ds(EVENTS + k, devices, stride=own), :]
+    loglik = jnp.sum(evidence, axis=0, keepdims=True) / jnp.float32(EVENTS)
+    out_ref[pl.ds(2 * own, devices, stride=out_stride), :] = jnp.broadcast_to(loglik, (devices, LANES))
+
+
+def merge(got, devices, tiles):
+    total = devices * tiles
+    f32 = jnp.float32
+    vmem = pl.BlockSpec(memory_space=pltpu.VMEM)
+    return pl.pallas_call(
+        functools.partial(merge_kernel, devices, tiles),
+        out_shape=jax.ShapeDtypeStruct((devices * (2 * (EVENTS // devices) + 1), LANES), f32),
+        in_specs=[vmem],
+        out_specs=vmem,
+        scratch_shapes=[pltpu.VMEM((total, LANES), f32)] * 5
+        + [pltpu.VMEM((EVENTS, LANES), f32), pltpu.VMEM((2 * EVENTS, LANES), f32)],
+    )(got)
+
+
+def last_kernel(devices, own, got_ref, evidence_ref, ess_ref, posterior_ref):
+    stride = 2 * own + 1
+    for d in range(devices):
+        lane = slice(d * LANES, (d + 1) * LANES)
+        evidence_ref[:, lane] = got_ref[d * stride : d * stride + own, :]
+        ess_ref[:, lane] = got_ref[d * stride + own : d * stride + 2 * own, :]
+    loglik = got_ref[pl.ds(2 * own, devices, stride=stride), :]
+    top = jnp.max(jnp.max(loglik, axis=0, keepdims=True), axis=1, keepdims=True)
+    mass = jnp.exp(loglik - top)
+    mass = jnp.sum(jnp.sum(mass, axis=0, keepdims=True), axis=1, keepdims=True)
+    posterior_ref[...] = loglik - (top + jnp.log(mass))
+
+
+def last(got, devices, own):
+    f32 = jnp.float32
+    vmem = pl.BlockSpec(memory_space=pltpu.VMEM)
+    cols = devices * LANES
+    return pl.pallas_call(
+        functools.partial(last_kernel, devices, own),
+        out_shape=(
+            jax.ShapeDtypeStruct((own, cols), f32),
+            jax.ShapeDtypeStruct((own, cols), f32),
+            jax.ShapeDtypeStruct((devices, LANES), f32),
+        ),
+        in_specs=[vmem],
+        out_specs=(vmem, vmem, vmem),
+    )(got)
+
+
+def exchange(x, devices):
+    width = x.shape[0] // devices * LANES
+    got = lax.all_to_all(x.reshape(devices, 1, width), "samp", split_axis=0, concat_axis=0, tiled=True)
+    return got.reshape(x.shape)
+
+
+def column_body(devices, summary, kernel, grid_offset, log_prior, tile_event, tile_live):
+    tiles = tile_event.shape[0]
+    own = EVENTS // devices
+    sent = tile_stats(summary, kernel, grid_offset, log_prior, tile_event, tile_live)
+    merged = merge(exchange(sent, devices), devices, tiles)
+    evidence, ess, posterior = last(exchange(merged, devices), devices, own)
+    return evidence, ess, posterior.reshape(-1)
+
+
+def row_body(summary, kernel, grid_offset, log_prior, tile_event, tile_live):
     row_count = summary.shape[0]
     grid_cols = kernel.shape[1]
     tile_count = tile_event.shape[0]
@@ -55,4 +377,13 @@
 def solution(mesh):
     in_specs = (P("samp", None), P(None, "grid"), P("grid"), P("samp"), P("samp"), P("samp"))
     out_specs = (P("samp", "grid"), P("samp", "grid"), P("grid"))
+    devices = mesh.shape["samp"]
+
+    def body(summary, kernel, *rest):
+        tile_rows = summary.shape[0] // rest[2].shape[0]
+        whole_lanes = kernel.shape[1] == devices * LANES and tile_rows == LANES
+        if mesh.shape["grid"] == 1 and whole_lanes:
+            return column_body(devices, summary, kernel, *rest)
+        return row_body(summary, kernel, *rest)
+
     return jax.shard_map(body, mesh=mesh, in_specs=in_specs, out_specs=out_specs, check_vma=False)

time: 202 us -> 89.4 us (0.44)
  waiting for transfers between devices: 71.9 us -> 0 us
  Pallas kernels: 0 us -> 39 us
  other arithmetic: 33.5 us -> 0 us
  matrix products: 27.1 us -> 0 us
  starting transfers between devices: 20.6 us -> 0 us
  blocking collectives: 38.6 us -> 44.9 us
  local copies, waits for them, and re-layouts: 7.87 us -> 4.9 us
    all_to_all x4 -> x0, waiting for transfers between devices: 71.9 us -> none  [the longest x1 24.3 us: body(): lax.all_to_all(local_second[:, None, :], 'samp', split_axis=0, concat_axi...]
    all_to_all x0 -> x2, blocking collectives: none -> 44.9 us  [exchange(): lax.all_to_all(x.reshape(devices, 1, width), 'samp', split_axis=0, concat...]
    pallas_call x0 -> x3, Pallas kernels: none -> 39 us  [the longest x1 30.7 us: tile_stats(): pl.pallas_call(functools.partial(stats_kernel, tiles, tile_rows, depth, c...]
    psum x1 -> x0, blocking collectives: 38.6 us -> none  [body(): lax.psum(jnp.sum(log_evidence, axis=0), 'samp') / jnp.float32(EVENTS)]
    dot_general x3 -> x0, matrix products: 27.1 us -> none  [the longest x1 25.7 us: body(): scores = jnp.dot(summary, kernel, preferred_element_type=jnp.float32)]
    reduce_sum x6 -> x0, other arithmetic: 23.1 us -> none  [the longest x1 17.1 us: body(): tile_second = jnp.sum(shifted * shifted, axis=1)]
    all_to_all x4 -> x0, starting transfers between devices: 20.6 us -> none  [the longest x1 7.33 us: body(): lax.all_to_all(live_count[:, None, None], 'samp', split_axis=0, concat_ax...]
    reduce_max x3 -> x0, other arithmetic: 7.1 us -> none  [the longest x1 5.55 us: body(): jnp.max(jnp.where(member[:, :, None], tile_max[None, :, :], jnp.float32(-...]
  transfers between devices with their start and end apart: 4 -> 0, of which waited for: 3 -> 0; matrix products, arithmetic and copies ran while one was open for 30% -> 0% of each run, Pallas kernels for 0% -> 0%
where the time goes in v1:
time: 89.4 us
  blocking collectives  44.9 us (50%)
  Pallas kernels  39 us (44%)
  local copies, waits for them, and re-layouts  4.9 us (5%)
    all_to_all x2, blocking collectives, exchange(): lax.all_to_all(x.reshape(devices, 1, width), 'samp', split_axis=0, concat...  44.9 us
    pallas_call x1, Pallas kernels, tile_stats(): pl.pallas_call(functools.partial(stats_kernel, tiles, tile_rows, depth, c...  30.7 us
    pallas_call x1, Pallas kernels, merge(): pl.pallas_call(functools.partial(merge_kernel, devices, tiles), out_shape...  6.65 us
    unnamed x10, local copies, waits for them, and re-layouts  4.9 us

profile of v1, /device:TPU:0, one launch (start us, length us, event | category | flops | bytes accessed | tf_op | source)
XLA Modules:
  0.0 89.4 jit_solution(9825485865157759458)
XLA Ops:
  0.6 0.0 copy-start
  0.6 2.2 %copy-done = bf16[2048,1024]{1,0:T(8,128)(2,1)S(1)} copy-done((bf16[2048,1024]{1,0:T(8,128)(2,1)S(1)}, bf16[2048,1024]{1,0:T(8,128)(2,1)}, u32[]{:S(2)}) %copy-start) | copy-done | bytes 4194328
  2.8 0.0 copy-start.1
  2.8 0.7 copy-done.1
  3.5 0.0 copy-start.2
  3.5 0.7 copy-done.2
  4.2 0.0 copy-start.3
  4.2 0.7 copy-done.3
  4.9 0.0 copy-start.4
  4.9 0.7 copy-done.4
  5.5 30.7 %shard_map.85 = f32[1056,128]{1,0:T(8,128)S(1)} custom-call(s32[16]{0:T(128)S(1)} %copy-done.3, s32[16]{0:T(128)S(1)} %copy-done.4, f32[1,4096]{1,0:T(1,128)S(1)} %bitcast.8, f32[16,128]{1,0:T(8,128)S(1)} %bitcast.9, bf16[2048,1024]{1,0:T(8,128)(2,1)S(1)} %copy-done, bf16[1024,4096]{1,0:T(8,128)(2,1)} %kernel_ref.1), custom_call_target="tpu_custom_call" | custom-call | tf_op jit(solution)/shard_map/pallas_call | solution.py:188
  36.2 34.0 %all_to_all.10 = f32[32,1,4224]{2,1,0:T(1,128)} all-to-all(f32[32,1,4224]{2,1,0:T(1,128)S(1)} %bitcast.7), channel_id=1, replica_groups=mesh['grid'=1,'samp'=32] {'samp'}, dimensions={0} | all-to-all | bytes 1081344 | tf_op jit(solution)/shard_map/all_to_all | solution.py:318
  70.3 6.6 %shard_map.86 = f32[160,128]{1,0:T(8,128)} custom-call(f32[1056,128]{1,0:T(8,128)} %bitcast.10), custom_call_target="tpu_custom_call" | custom-call | tf_op jit(solution)/shard_map/pallas_call | solution.py:277
  76.9 10.8 %all_to_all.11 = f32[32,1,640]{2,1,0:T(1,128)} all-to-all(f32[32,1,640]{2,1,0:T(1,128)} %bitcast.11), channel_id=1, replica_groups=mesh['grid'=1,'samp'=32] {'samp'}, dimensions={0} | all-to-all | bytes 163840 | tf_op jit(solution)/shard_map/all_to_all | solution.py:318
  87.8 1.7 %shard_map.87 = (f32[2,4096]{1,0:T(2,128)}, f32[2,4096]{1,0:T(2,128)}, f32[32,128]{1,0:T(8,128)}) custom-call(f32[160,128]{1,0:T(8,128)} %bitcast.12), custom_call_target="tpu_custom_call" | custom-call | tf_op jit(solution)/shard_map/pallas_call | solution.py:304
Async XLA Ops:
  0.6 2.2 %copy-start = (bf16[2048,1024]{1,0:T(8,128)(2,1)S(1)}, bf16[2048,1024]{1,0:T(8,128)(2,1)}, u32[]{:S(2)}) copy-start(bf16[2048,1024]{1,0:T(8,128)(2,1)} %summary_ref.1) | copy-start | bytes 12582916
  2.8 0.7 copy-start.1
  3.5 0.7 copy-start.2
  4.2 0.7 copy-start.3
  4.9 0.7 copy-start.4

commit v2 on v1

--- a/solution.py
+++ b/solution.py
@@ -11,19 +11,39 @@
 LANES = 128
 GROUP = 16
 CHUNK = 256
-BLOCK = 512
+BLOCK = 1024
 NEG = -1e30
 DEAD = 1e30
 
 
 def stats_kernel(
-    tiles, tile_rows, depth, cols, event_ref, live_ref, offset_ref, prior_ref, summary_ref, kernel_ref,
-    out_ref, lhs, rhs, prior, score_a, score_b, top, peak, first, second, owner, start, row_sem, col_sem,
+    tiles, tile_rows, depth, cols, event_hbm, live_hbm, offset_hbm, prior_hbm, summary_ref, kernel_ref,
+    out_ref, lhs, rhs, prior, score_a, score_b, top, peak, held_sums, offset_ref, prior_ref,
+    event_ref, live_ref, owner, fresh, start, row_sem, col_sem, fact_sem,
 ):
     blocks = cols // BLOCK
     per_tile = tile_rows // GROUP
     sizes = [1 << k for k in reversed(range(per_tile.bit_length()))]
     stride = 2 * tiles + 1
+    lanes = BLOCK // LANES
+    span = 8 * tiles + 8
+    peak_span = tiles + 8
+    parts = lanes // 2
+    chunk_groups = CHUNK // GROUP
+
+    facts = [
+        pltpu.make_async_copy(source, target, fact_sem.at[k])
+        for k, (source, target) in enumerate(
+            ((live_hbm, live_ref), (event_hbm, event_ref), (prior_hbm, prior_ref), (offset_hbm, offset_ref))
+        )
+    ]
+    for copy in facts:
+        copy.start()
+
+    def col_copy(n):
+        return pltpu.make_async_copy(kernel_ref.at[:, pl.ds(n * BLOCK, BLOCK)], rhs.at[n], col_sem.at[n])
+
+    col_copy(0).start()
 
     def row_copies(act):
         for t in range(tiles):
@@ -41,24 +61,24 @@
                     )
                     act(copy)
 
-    def col_copy(n):
-        return pltpu.make_async_copy(kernel_ref.at[:, pl.ds(n * BLOCK, BLOCK)], rhs.at[n], col_sem.at[n])
-
+    facts[0].wait()
     total = jnp.int32(0)
     for t in range(tiles):
         start[t] = total
         total = total + lax.div(live_ref[t] + (GROUP - 1), GROUP)
     row_copies(lambda copy: copy.start())
-    for n in range(blocks):
+    for n in range(1, blocks):
         col_copy(n).start()
-
-    chunk_groups = CHUNK // GROUP
+    for copy in facts[1:]:
+        copy.wait()
+
     chunks = lax.div(total + (chunk_groups - 1), chunk_groups)
     for t in range(tiles):
         count = lax.div(live_ref[t] + (GROUP - 1), GROUP)
 
         def mark(j, carry):
             owner[start[t] + j] = t
+            fresh[start[t] + j] = jnp.where(j == 0, jnp.float32(0), jnp.float32(1))
             return carry
 
         lax.fori_loop(0, count, mark, 0)
@@ -68,68 +88,74 @@
         prior[pl.ds(pl.multiple_of(start[t] * GROUP, GROUP), tile_rows), :] = spread
     for j in range(chunk_groups):
         owner[total + j] = tiles
-
-    top[...] = jnp.full(top.shape, NEG, jnp.float32)
-    first[...] = jnp.zeros(first.shape, jnp.float32)
-    second[...] = jnp.zeros(second.shape, jnp.float32)
+        fresh[total + j] = jnp.float32(0)
+
+    top[...] = jnp.zeros(top.shape, jnp.float32)
+    held_sums[...] = jnp.zeros(held_sums.shape, jnp.float32)
     peak[...] = jnp.zeros(peak.shape, jnp.float32)
     row_copies(lambda copy: copy.wait())
 
-    def slot_of(tile, w):
-        return pl.ds(pl.multiple_of(tile * 8 + w * (8 * tiles + 8), 8), 8)
-
-    def products(n, c, score):
-        row = pl.multiple_of(c * CHUNK, CHUNK)
-        rows = lhs[pl.ds(row, CHUNK), :]
-        for h in range(BLOCK // 256):
-            part = jnp.dot(rows, rhs[n, :, h * 256 : (h + 1) * 256], preferred_element_type=jnp.float32)
-            for g in range(chunk_groups):
-                at = pl.ds(pl.multiple_of(row + g * GROUP, GROUP), GROUP)
-                held = prior[at, :]
-                for w in range(256 // LANES):
-                    lane = pl.ds(h * 256 + w * LANES, LANES)
-                    slot = slot_of(owner[c * chunk_groups + g], h * 2 + w)
-                    value = part[g * GROUP : (g + 1) * GROUP, w * LANES : (w + 1) * LANES] - held
-                    score[at, lane] = value
-                    top[slot, :] = jnp.maximum(top[slot, :], jnp.maximum(value[:8], value[8:]))
-
-    def sums(c, score):
-        row = pl.multiple_of(c * CHUNK, CHUNK)
+    def rows_at(c, g):
+        return pl.ds(pl.multiple_of(c * CHUNK, CHUNK) + g * GROUP, GROUP)
+
+    def products(n, c, score, h):
+        rows = lhs[pl.ds(pl.multiple_of(c * CHUNK, CHUNK), CHUNK), :]
+        part = jnp.dot(rows, rhs[n, :, h * 256 : (h + 1) * 256], preferred_element_type=jnp.float32)
+        base = pl.multiple_of(owner[c * chunk_groups] * 8, 8)
+        held = [top[pl.ds(base + (h * 2 + w) * span, 8), :] for w in range(2)]
         for g in range(chunk_groups):
-            at = pl.ds(pl.multiple_of(row + g * GROUP, GROUP), GROUP)
+            base = pl.multiple_of(owner[c * chunk_groups + g] * 8, 8)
+            reset = fresh[c * chunk_groups + g] * jnp.float32(DEAD) - jnp.float32(DEAD)
+            cost = prior[rows_at(c, g), :]
+            for w in range(2):
+                lane = h * 2 + w
+                value = part[g * GROUP : (g + 1) * GROUP, w * LANES : (w + 1) * LANES] - cost
+                score[rows_at(c, g), lane * LANES : (lane + 1) * LANES] = value
+                held[w] = jnp.maximum(held[w] + reset, jnp.maximum(value[:8], value[8:]))
+                top[pl.ds(base + lane * span, 8), :] = held[w]
+
+    def sums_open(c):
+        base = pl.multiple_of(owner[c * chunk_groups] * 8, 8)
+        return [
+            [held_sums[pl.ds(base + (k * lanes + lane) * span, 8), :] for lane in range(lanes)] for k in range(2)
+        ]
+
+    def sums(c, score, part, held):
+        one, two = held
+        for g in range(part * chunk_groups // parts, (part + 1) * chunk_groups // parts):
             tile = owner[c * chunk_groups + g]
-            for w in range(BLOCK // LANES):
-                slot = slot_of(tile, w)
-                level = peak[pl.ds(tile + w * (tiles + 8), 8, stride=0), :]
-                value = score[at, pl.ds(w * LANES, LANES)]
+            base = pl.multiple_of(tile * 8, 8)
+            keep = fresh[c * chunk_groups + g]
+            for lane in range(lanes):
+                level = peak[pl.ds(tile + lane * peak_span, 8, stride=0), :]
+                value = score[rows_at(c, g), lane * LANES : (lane + 1) * LANES]
                 low, high = jnp.exp(value[:8] - level), jnp.exp(value[8:] - level)
-                first[slot, :] = first[slot, :] + (low + high)
-                second[slot, :] = second[slot, :] + (low * low + high * high)
+                one[lane] = one[lane] * keep + (low + high)
+                two[lane] = two[lane] * keep + (low * low + high * high)
+                held_sums[pl.ds(base + lane * span, 8), :] = one[lane]
+                held_sums[pl.ds(base + (lanes + lane) * span, 8), :] = two[lane]
 
     def fold(ref, half, w, join):
-        parts = [ref[pl.ds(w * (8 * tiles + 8) + half * 64 + i, 8, stride=8), :] for i in range(8)]
-        while len(parts) > 1:
-            parts = [join(a, b) for a, b in zip(parts[::2], parts[1::2])]
-        return parts[0]
+        kept = [ref[pl.ds(w * span + half * 64 + i, 8, stride=8), :] for i in range(8)]
+        while len(kept) > 1:
+            kept = [join(a, b) for a, b in zip(kept[::2], kept[1::2])]
+        return kept[0]
 
     def close_top():
         for half in range(tiles // 8):
-            for w in range(BLOCK // LANES):
-                peak[pl.ds(w * (tiles + 8) + half * 8, 8), :] = fold(top, half, w, jnp.maximum)
-        top[...] = jnp.full(top.shape, NEG, jnp.float32)
+            for w in range(lanes):
+                peak[pl.ds(w * peak_span + half * 8, 8), :] = fold(top, half, w, jnp.maximum)
 
     def close_sums(n):
         for half in range(tiles // 8):
-            for w in range(BLOCK // LANES):
-                one = fold(first, half, w, jnp.add)
-                two = fold(second, half, w, jnp.add)
-                level = peak[pl.ds(w * (tiles + 8) + half * 8, 8), :]
+            for w in range(lanes):
+                one = fold(held_sums, half, w, jnp.add)
+                two = fold(held_sums, half, lanes + w, jnp.add)
+                level = peak[pl.ds(w * peak_span + half * 8, 8), :]
                 shift = offset_ref[:, pl.ds(pl.multiple_of(n * BLOCK + w * LANES, LANES), LANES)]
-                base = (n * (BLOCK // LANES) + w) * stride + half * 8
+                base = (n * lanes + w) * stride + half * 8
                 out_ref[pl.ds(base, 8), :] = level + jnp.log(one) + shift
                 out_ref[pl.ds(base + tiles, 8), :] = two / (one * one)
-        first[...] = jnp.zeros(first.shape, jnp.float32)
-        second[...] = jnp.zeros(second.shape, jnp.float32)
 
     def each_chunk(work):
         def step(c, carry):
@@ -138,16 +164,27 @@
 
         lax.fori_loop(0, chunks, step, 0)
 
+    def only_products(c):
+        for h in range(lanes // 2):
+            products(0, c, score_a, h)
+
+    def only_sums(c):
+        held = sums_open(c)
+        for h in range(parts):
+            sums(c, score_b, h, held)
+
     col_copy(0).wait()
-    each_chunk(lambda c: products(0, c, score_a))
+    each_chunk(only_products)
 
     def step(n, now, before):
         close_top()
         col_copy(n).wait()
 
         def work(c):
-            products(n, c, now)
-            sums(c, before)
+            held = sums_open(c)
+            for h in range(parts):
+                sums(c, before, h, held)
+                products(n, c, now, h)
 
         each_chunk(work)
         close_sums(n - 1)
@@ -163,7 +200,7 @@
 
     lax.fori_loop(0, blocks // 2, pair, 0)
     close_top()
-    each_chunk(lambda c: sums(c, score_b))
+    each_chunk(only_sums)
     close_sums(blocks - 1)
 
     lane_at = lax.broadcasted_iota(jnp.int32, (1, LANES), 1)
@@ -181,31 +218,36 @@
     tiles = tile_event.shape[0]
     tile_rows = rows // tiles
     stride = 2 * tiles + 1
-    smem = pl.BlockSpec(memory_space=pltpu.SMEM)
-    vmem = pl.BlockSpec(memory_space=pltpu.VMEM)
-    hbm = pl.BlockSpec(memory_space=pl.ANY)
+    hbm = pl.BlockSpec(memory_space=pltpu.HBM)
     f32 = jnp.float32
+    lanes = BLOCK // LANES
+    groups = (rows + CHUNK) // GROUP
     return pl.pallas_call(
         functools.partial(stats_kernel, tiles, tile_rows, depth, cols),
         out_shape=jax.ShapeDtypeStruct((cols // LANES * stride, LANES), f32),
-        in_specs=[smem, smem, vmem, vmem, hbm, hbm],
-        out_specs=vmem,
+        in_specs=[hbm] * 6,
+        out_specs=pl.BlockSpec(memory_space=pltpu.VMEM),
         scratch_shapes=[
             pltpu.VMEM((rows + CHUNK, depth), jnp.bfloat16),
             pltpu.VMEM((cols // BLOCK, depth, BLOCK), jnp.bfloat16),
             pltpu.VMEM((rows + CHUNK, LANES), f32),
             pltpu.VMEM((rows + CHUNK, BLOCK), f32),
             pltpu.VMEM((rows + CHUNK, BLOCK), f32),
-            pltpu.VMEM((BLOCK // LANES * (8 * tiles + 8), LANES), f32),
-            pltpu.VMEM((BLOCK // LANES * (tiles + 8), LANES), f32),
-            pltpu.VMEM((BLOCK // LANES * (8 * tiles + 8), LANES), f32),
-            pltpu.VMEM((BLOCK // LANES * (8 * tiles + 8), LANES), f32),
-            pltpu.SMEM((rows // GROUP + CHUNK // GROUP,), jnp.int32),
+            pltpu.VMEM((lanes * (8 * tiles + 8), LANES), f32),
+            pltpu.VMEM((lanes * (tiles + 8), LANES), f32),
+            pltpu.VMEM((2 * lanes * (8 * tiles + 8), LANES), f32),
+            pltpu.VMEM((1, cols), f32),
+            pltpu.VMEM((tiles, tile_rows), f32),
+            pltpu.SMEM((tiles,), jnp.int32),
+            pltpu.SMEM((tiles,), jnp.int32),
+            pltpu.SMEM((groups,), jnp.int32),
+            pltpu.SMEM((groups,), f32),
             pltpu.SMEM((tiles,), jnp.int32),
             pltpu.SemaphoreType.DMA((tiles, (tile_rows // GROUP).bit_length())),
             pltpu.SemaphoreType.DMA((cols // BLOCK,)),
+            pltpu.SemaphoreType.DMA((4,)),
         ],
-        compiler_params=pltpu.CompilerParams(vmem_limit_bytes=48 << 20),
+        compiler_params=pltpu.CompilerParams(vmem_limit_bytes=56 << 20),
     )(
         tile_event, tile_live, grid_offset.reshape(1, cols), log_prior.reshape(tiles, tile_rows), summary, kernel,
     )

time: 89.4 us -> 72.9 us (0.82)
  Pallas kernels: 39 us -> 30.3 us
  local copies, waits for them, and re-layouts: 4.9 us -> 0 us
  blocking collectives: 44.9 us -> 41.8 us
    pallas_call x1, Pallas kernels: 30.7 us -> 22 us  [tile_stats(): pl.pallas_call(functools.partial(stats_kernel, tiles, tile_rows, depth, c...]
    unnamed x10 -> x0, local copies, waits for them, and re-layouts: 4.9 us -> none
    all_to_all x2, blocking collectives: 44.9 us -> 41.8 us  [exchange(): lax.all_to_all(x.reshape(devices, 1, width), 'samp', split_axis=0, concat...]
where the time goes in v2:
time: 72.9 us; the launch traced here: 72.8 us
  blocking collectives  41.8 us (57%)
  Pallas kernels  30.3 us (42%)
    all_to_all x2, blocking collectives, exchange(): lax.all_to_all(x.reshape(devices, 1, width), 'samp', split_axis=0, concat...  41.8 us
    pallas_call x1, Pallas kernels, tile_stats(): pl.pallas_call(functools.partial(stats_kernel, tiles, tile_rows, depth, c...  22 us
    pallas_call x1, Pallas kernels, merge(): pl.pallas_call(functools.partial(merge_kernel, devices, tiles), out_shape...  6.65 us
    pallas_call x1, Pallas kernels, last(): pl.pallas_call(functools.partial(last_kernel, devices, own), out_shape=(j...  1.68 us

profile of v2, /device:TPU:0, one launch (start us, length us, event | category | flops | bytes accessed | tf_op | source)
XLA Modules:
  0.0 72.8 jit_solution(1109689066267342668)
XLA Ops:
  0.6 22.0 %shard_map.85 = f32[1056,128]{1,0:T(8,128)} custom-call(s32[16]{0:T(128)} %event_hbm.1, s32[16]{0:T(128)} %live_hbm.1, f32[1,4096]{1,0:T(1,128)} %bitcast.11, f32[16,128]{1,0:T(8,128)} %bitcast.12, bf16[2048,1024]{1,0:T(8,128)(2,1)} %summary_ref.1, bf16[1024,4096]{1,0:T(8,128)(2,1)} %kernel_ref.1), custom_call_target="tpu_custom_call" | custom-call | tf_op jit(solution)/shard_map/pallas_call | solution.py:225
  22.6 31.0 %all_to_all.10 = f32[32,1,4224]{2,1,0:T(1,128)} all-to-all(f32[32,1,4224]{2,1,0:T(1,128)} %bitcast.7), channel_id=1, replica_groups=mesh['grid'=1,'samp'=32] {'samp'}, dimensions={0} | all-to-all | bytes 1081344 | tf_op jit(solution)/shard_map/all_to_all | solution.py:360
  53.6 6.7 %shard_map.86 = f32[160,128]{1,0:T(8,128)} custom-call(f32[1056,128]{1,0:T(8,128)} %bitcast.8), custom_call_target="tpu_custom_call" | custom-call | tf_op jit(solution)/shard_map/pallas_call | solution.py:319
  60.2 10.8 %all_to_all.11 = f32[32,1,640]{2,1,0:T(1,128)} all-to-all(f32[32,1,640]{2,1,0:T(1,128)} %bitcast.9), channel_id=1, replica_groups=mesh['grid'=1,'samp'=32] {'samp'}, dimensions={0} | all-to-all | bytes 163840 | tf_op jit(solution)/shard_map/all_to_all | solution.py:360
  71.1 1.7 %shard_map.87 = (f32[2,4096]{1,0:T(2,128)}, f32[2,4096]{1,0:T(2,128)}, f32[32,128]{1,0:T(8,128)}) custom-call(f32[160,128]{1,0:T(8,128)} %bitcast.10), custom_call_target="tpu_custom_call" | custom-call | tf_op jit(solution)/shard_map/pallas_call | solution.py:346

commit v3 on v2

--- a/solution.py
+++ b/solution.py
@@ -9,6 +9,7 @@
 
 EVENTS = 64
 LANES = 128
+HALF = 64
 GROUP = 16
 CHUNK = 256
 BLOCK = 1024
@@ -17,14 +18,15 @@
 
 
 def stats_kernel(
-    tiles, tile_rows, depth, cols, event_hbm, live_hbm, offset_hbm, prior_hbm, summary_ref, kernel_ref,
+    tiles, tile_rows, cols, column, facts_row, event_hbm, live_hbm, offset_hbm, prior_hbm, summary_ref, kernel_ref,
     out_ref, lhs, rhs, prior, score_a, score_b, top, peak, held_sums, offset_ref, prior_ref,
     event_ref, live_ref, owner, fresh, start, row_sem, col_sem, fact_sem,
 ):
     blocks = cols // BLOCK
     per_tile = tile_rows // GROUP
     sizes = [1 << k for k in reversed(range(per_tile.bit_length()))]
-    stride = 2 * tiles + 1
+    half_tiles = tiles // 2
+    stride = tiles + facts_row
     lanes = BLOCK // LANES
     span = 8 * tiles + 8
     peak_span = tiles + 8
@@ -41,7 +43,7 @@
         copy.start()
 
     def col_copy(n):
-        return pltpu.make_async_copy(kernel_ref.at[:, pl.ds(n * BLOCK, BLOCK)], rhs.at[n], col_sem.at[n])
+        return pltpu.make_async_copy(kernel_ref.at[:, pl.ds(column + n * BLOCK, BLOCK)], rhs.at[n], col_sem.at[n])
 
     col_copy(0).start()
 
@@ -146,16 +148,23 @@
             for w in range(lanes):
                 peak[pl.ds(w * peak_span + half * 8, 8), :] = fold(top, half, w, jnp.maximum)
 
+    left = lax.broadcasted_iota(jnp.int32, (8, LANES), 1) < HALF
+
     def close_sums(n):
-        for half in range(tiles // 8):
-            for w in range(lanes):
+        for w in range(lanes):
+            shift = offset_ref[:, pl.ds(pl.multiple_of(column + n * BLOCK + w * LANES, LANES), LANES)]
+            values = []
+            for half in range(tiles // 8):
                 one = fold(held_sums, half, w, jnp.add)
                 two = fold(held_sums, half, lanes + w, jnp.add)
                 level = peak[pl.ds(w * peak_span + half * 8, 8), :]
-                shift = offset_ref[:, pl.ds(pl.multiple_of(n * BLOCK + w * LANES, LANES), LANES)]
-                base = (n * lanes + w) * stride + half * 8
-                out_ref[pl.ds(base, 8), :] = level + jnp.log(one) + shift
-                out_ref[pl.ds(base + tiles, 8), :] = two / (one * one)
+                values.append((level + jnp.log(one) + shift, two / (one * one)))
+            for part in range(half_tiles // 8):
+                for k in range(2):
+                    low, high = values[part][k], values[half_tiles // 8 + part][k]
+                    base = 2 * (n * lanes + w) * stride + k * half_tiles + part * 8
+                    out_ref[pl.ds(base, 8), :] = jnp.where(left, low, pltpu.roll(high, HALF, 1))
+                    out_ref[pl.ds(base + stride, 8), :] = jnp.where(left, pltpu.roll(low, HALF, 1), high)
 
     def each_chunk(work):
         def step(c, carry):
@@ -203,28 +212,30 @@
     each_chunk(only_sums)
     close_sums(blocks - 1)
 
-    lane_at = lax.broadcasted_iota(jnp.int32, (1, LANES), 1)
-    facts = jnp.zeros((1, LANES), jnp.float32)
-    for t in range(tiles):
-        facts = jnp.where(lane_at == t, event_ref[t].astype(jnp.float32), facts)
-        facts = jnp.where(lane_at == tiles + t, live_ref[t].astype(jnp.float32), facts)
-    for d in range(cols // LANES):
-        out_ref[d * stride + 2 * tiles : d * stride + 2 * tiles + 1, :] = facts
-
-
-def tile_stats(summary, kernel, grid_offset, log_prior, tile_event, tile_live):
+    if facts_row:
+        lane_at = lax.broadcasted_iota(jnp.int32, (1, LANES), 1)
+        facts = jnp.zeros((1, LANES), jnp.float32)
+        for t in range(tiles):
+            facts = jnp.where(lane_at == t, event_ref[t].astype(jnp.float32), facts)
+            facts = jnp.where(lane_at == tiles + t, live_ref[t].astype(jnp.float32), facts)
+        for d in range(cols // HALF):
+            out_ref[d * stride + tiles : d * stride + tiles + 1, :] = facts
+
+
+def tile_stats(summary, kernel, grid_offset, log_prior, tile_event, tile_live, part):
     rows, depth = summary.shape
-    cols = kernel.shape[1]
+    cols = kernel.shape[1] // 2
+    facts_row = 1 - part
     tiles = tile_event.shape[0]
     tile_rows = rows // tiles
-    stride = 2 * tiles + 1
+    stride = tiles + facts_row
     hbm = pl.BlockSpec(memory_space=pltpu.HBM)
     f32 = jnp.float32
     lanes = BLOCK // LANES
     groups = (rows + CHUNK) // GROUP
     return pl.pallas_call(
-        functools.partial(stats_kernel, tiles, tile_rows, depth, cols),
-        out_shape=jax.ShapeDtypeStruct((cols // LANES * stride, LANES), f32),
+        functools.partial(stats_kernel, tiles, tile_rows, cols, part * cols, facts_row),
+        out_shape=jax.ShapeDtypeStruct((cols // HALF * stride, LANES), f32),
         in_specs=[hbm] * 6,
         out_specs=pl.BlockSpec(memory_space=pltpu.VMEM),
         scratch_shapes=[
@@ -236,7 +247,7 @@
             pltpu.VMEM((lanes * (8 * tiles + 8), LANES), f32),
             pltpu.VMEM((lanes * (tiles + 8), LANES), f32),
             pltpu.VMEM((2 * lanes * (8 * tiles + 8), LANES), f32),
-            pltpu.VMEM((1, cols), f32),
+            pltpu.VMEM((1, 2 * cols), f32),
             pltpu.VMEM((tiles, tile_rows), f32),
             pltpu.SMEM((tiles,), jnp.int32),
             pltpu.SMEM((tiles,), jnp.int32),
@@ -247,9 +258,10 @@
             pltpu.SemaphoreType.DMA((cols // BLOCK,)),
             pltpu.SemaphoreType.DMA((4,)),
         ],
-        compiler_params=pltpu.CompilerParams(vmem_limit_bytes=56 << 20),
+        cost_estimate=pl.CostEstimate(flops=rows * depth * cols, bytes_accessed=4 * rows * depth, transcendentals=0),
+        compiler_params=pltpu.CompilerParams(vmem_limit_bytes=60 << 20),
     )(
-        tile_event, tile_live, grid_offset.reshape(1, cols), log_prior.reshape(tiles, tile_rows), summary, kernel,
+        tile_event, tile_live, grid_offset.reshape(1, 2 * cols), log_prior.reshape(tiles, tile_rows), summary, kernel,
     )
 
 
@@ -261,48 +273,98 @@
     return high, middle, low
 
 
-def merge_kernel(devices, tiles, got_ref, out_ref, level, event, ratio, live, peak_of, peak, kept):
-    stride = 2 * tiles + 1
-    total = devices * tiles
-    facts = got_ref[pl.ds(2 * tiles, devices, stride=stride), :]
-    for i in range(tiles):
+def swap(x):
+    return pltpu.roll(x, HALF, 1)
+
+
+def join_events(level, event, chosen, ratio, peak):
+    total = level.shape[0]
+    peak[...] = jnp.zeros(peak.shape, jnp.float32)
+
+    def find(step, carry):
+        names = [(step * 4 + k).astype(jnp.float32) for k in range(4)]
+        parts = [[jnp.full((8, LANES), NEG, jnp.float32) for _ in range(2)] for _ in range(4)]
+        for v in range(total // 8):
+            at = slice(v * 8, v * 8 + 8)
+            whose, value = event[at, :], level[at, :]
+            for k in range(4):
+                parts[k][v % 2] = jnp.maximum(
+                    parts[k][v % 2], jnp.where(whose == names[k], value, jnp.float32(NEG))
+                )
+        for k in range(4):
+            best = jnp.max(jnp.maximum(parts[k][0], parts[k][1]), axis=0, keepdims=True)
+            peak[pl.ds(step * 4 + k, 1), :] = jnp.maximum(best, swap(best))
+        return carry
+
+    lax.fori_loop(0, EVENTS // 4, find, 0)
+    left = lax.broadcasted_iota(jnp.int32, (total, LANES), 1) < HALF
+    found = jnp.dot(chosen, jnp.concatenate(split3(peak[...]), axis=1), preferred_element_type=jnp.float32)
+    found = (found[:, :LANES] + found[:, LANES : 2 * LANES]) + found[:, 2 * LANES :]
+    one = jnp.exp(level[...] - jnp.where(left, found[:total], found[total:]))
+    two = ratio * one * one
+    pieces = []
+    for side in (left, ~left):
+        pieces.append(jnp.concatenate(
+            split3(jnp.where(side, one, jnp.float32(0))) + split3(jnp.where(side, two, jnp.float32(0))), axis=1
+        ))
+    right = jnp.concatenate(pieces, axis=0)
+    sums = lax.dot_general(chosen, right, (((0,), (0,)), ((), ())), preferred_element_type=jnp.float32)
+    part = [sums[:EVENTS, k * LANES : (k + 1) * LANES] for k in range(6)]
+    first = (part[0] + part[1]) + part[2]
+    second = (part[3] + part[4]) + part[5]
+    return peak[:EVENTS, :], first + swap(first), second + swap(second)
+
+
+def choose(low, high):
+    names = lax.broadcasted_iota(jnp.int32, low.shape, 1).astype(jnp.float32)
+    both = jnp.concatenate([low, high], axis=0)
+    names = jnp.concatenate([names, names], axis=0)
+    return jnp.where(both == names, jnp.float32(1), jnp.float32(0)).astype(jnp.bfloat16)
+
+
+def merge_first_kernel(devices, tiles, got_ref, done_ref, event_ref, level, event, peak):
+    half = tiles // 2
+    stride = tiles + 1
+    total = devices * half
+    facts = got_ref[pl.ds(tiles, devices, stride=stride), :]
+    left = lax.broadcasted_iota(jnp.int32, (devices, LANES), 1) < HALF
+    live = []
+    for k in range(2):
+        for i in range(half):
+            t = k * half + i
+            spread = jnp.broadcast_to(facts[:, t : t + 1], (devices, LANES))
+            event_ref[(k * half + i) * devices : (k * half + i + 1) * devices, :] = spread
+            live.append(jnp.broadcast_to(facts[:, tiles + t : tiles + t + 1], (devices, LANES)))
+    for i in range(half):
         at = slice(i * devices, (i + 1) * devices)
         level[at, :] = got_ref[pl.ds(i, devices, stride=stride), :]
-        ratio[at, :] = got_ref[pl.ds(tiles + i, devices, stride=stride), :]
-        event[at, :] = jnp.broadcast_to(facts[:, i : i + 1], (devices, LANES))
-        live[at, :] = jnp.broadcast_to(facts[:, tiles + i : tiles + i + 1], (devices, LANES))
-
-    def find(e, carry):
-        name = e.astype(jnp.float32)
-        parts = [jnp.full((8, LANES), NEG, jnp.float32) for _ in range(4)]
-        for v in range(total // 8):
-            at = slice(v * 8, v * 8 + 8)
-            parts[v % 4] = jnp.maximum(
-                parts[v % 4], jnp.where(event[at, :] == name, level[at, :], jnp.float32(NEG))
-            )
-        best = jnp.maximum(jnp.maximum(parts[0], parts[1]), jnp.maximum(parts[2], parts[3]))
-        best = jnp.max(best, axis=0, keepdims=True)
-        peak[pl.ds(e, 1), :] = best
-        wide = jnp.broadcast_to(best, (8, LANES))
-        for v in range(total // 8):
-            at = slice(v * 8, v * 8 + 8)
-            peak_of[at, :] = jnp.where(event[at, :] == name, wide, peak_of[at, :])
-        return carry
-
-    lax.fori_loop(0, EVENTS, find, 0)
-    one = jnp.exp(level[...] - peak_of[...])
-    two = ratio[...] * one * one
-    lanes = lax.broadcasted_iota(jnp.int32, (total, LANES), 1).astype(jnp.float32)
-    chosen = jnp.where(event[...] == lanes, jnp.float32(1), jnp.float32(0)).astype(jnp.bfloat16)
-    right = jnp.concatenate(split3(one) + split3(two) + (live[...].astype(jnp.bfloat16),), axis=1)
-    sums = lax.dot_general(chosen, right, (((0,), (0,)), ((), ())), preferred_element_type=jnp.float32)
-    part = [sums[:EVENTS, k * LANES : (k + 1) * LANES] for k in range(7)]
-    first = part[0] + part[1] + part[2]
-    second = part[3] + part[4] + part[5]
-    count = part[6]
-    evidence = peak[...] + jnp.log(first) - jnp.log(count)
+        event[at, :] = jnp.where(left, event_ref[at, :], event_ref[total + i * devices : total + (i + 1) * devices, :])
+    ratio = jnp.concatenate([got_ref[pl.ds(half + i, devices, stride=stride), :] for i in range(half)], axis=0)
+    chosen = choose(event_ref[:total, :], event_ref[total:, :])
+    top, first, second = join_events(level, event, chosen, ratio, peak)
+    live = jnp.concatenate(live, axis=0).astype(jnp.bfloat16)
+    count = lax.dot_general(chosen, live, (((0,), (0,)), ((), ())), preferred_element_type=jnp.float32)[:EVENTS]
+    done_ref[:EVENTS, :] = top + jnp.log(first) - jnp.log(count)
+    done_ref[EVENTS : 2 * EVENTS, :] = first * first / (second * count)
+    done_ref[2 * EVENTS :, :] = count
+
+
+def merge_second_kernel(devices, tiles, got_ref, done_ref, event_ref, out_ref, level, event, peak, kept):
+    half = tiles // 2
+    total = devices * half
+    left = lax.broadcasted_iota(jnp.int32, (devices, LANES), 1) < HALF
+    for i in range(half):
+        at = slice(i * devices, (i + 1) * devices)
+        level[at, :] = got_ref[pl.ds(i, devices, stride=tiles), :]
+        event[at, :] = jnp.where(left, event_ref[at, :], event_ref[total + i * devices : total + (i + 1) * devices, :])
+    ratio = jnp.concatenate([got_ref[pl.ds(half + i, devices, stride=tiles), :] for i in range(half)], axis=0)
+    chosen = choose(event_ref[:total, :], event_ref[total:, :])
+    top, first, second = join_events(level, event, chosen, ratio, peak)
+    count = done_ref[2 * EVENTS :, :]
+    left = lax.broadcasted_iota(jnp.int32, (EVENTS, LANES), 1) < HALF
+    evidence = jnp.where(left, done_ref[:EVENTS, :], top + jnp.log(first) - jnp.log(count))
     kept[:EVENTS, :] = evidence
-    kept[EVENTS:, :] = first * first / (second * count)
+    kept[EVENTS:, :] = jnp.where(left, done_ref[EVENTS : 2 * EVENTS, :], first * first / (second * count))
     own = EVENTS // devices
     out_stride = 2 * own + 1
     for k in range(own):
@@ -312,27 +374,57 @@
     out_ref[pl.ds(2 * own, devices, stride=out_stride), :] = jnp.broadcast_to(loglik, (devices, LANES))
 
 
-def merge(got, devices, tiles):
-    total = devices * tiles
+def merge_first(got, devices, tiles):
     f32 = jnp.float32
     vmem = pl.BlockSpec(memory_space=pltpu.VMEM)
+    total = devices * tiles // 2
     return pl.pallas_call(
-        functools.partial(merge_kernel, devices, tiles),
+        functools.partial(merge_first_kernel, devices, tiles),
+        out_shape=(
+            jax.ShapeDtypeStruct((3 * EVENTS, LANES), f32),
+            jax.ShapeDtypeStruct((2 * total, LANES), f32),
+        ),
+        in_specs=[vmem],
+        out_specs=(vmem, vmem),
+        scratch_shapes=[pltpu.VMEM((total, LANES), f32), pltpu.VMEM((total, LANES), f32), pltpu.VMEM((LANES, LANES), f32)],
+        cost_estimate=pl.CostEstimate(flops=400_000_000, bytes_accessed=1_000_000, transcendentals=0),
+        compiler_params=pltpu.CompilerParams(vmem_limit_bytes=8 << 20),
+    )(got)
+
+
+def merge_second(got, done, event, devices, tiles):
+    f32 = jnp.float32
+    vmem = pl.BlockSpec(memory_space=pltpu.VMEM)
+    total = devices * tiles // 2
+    return pl.pallas_call(
+        functools.partial(merge_second_kernel, devices, tiles),
         out_shape=jax.ShapeDtypeStruct((devices * (2 * (EVENTS // devices) + 1), LANES), f32),
-        in_specs=[vmem],
+        in_specs=[vmem] * 3,
         out_specs=vmem,
-        scratch_shapes=[pltpu.VMEM((total, LANES), f32)] * 5
-        + [pltpu.VMEM((EVENTS, LANES), f32), pltpu.VMEM((2 * EVENTS, LANES), f32)],
-    )(got)
+        scratch_shapes=[
+            pltpu.VMEM((total, LANES), f32),
+            pltpu.VMEM((total, LANES), f32),
+            pltpu.VMEM((LANES, LANES), f32),
+            pltpu.VMEM((2 * EVENTS, LANES), f32),
+        ],
+        compiler_params=pltpu.CompilerParams(vmem_limit_bytes=8 << 20),
+    )(got, done, event)
 
 
 def last_kernel(devices, own, got_ref, evidence_ref, ess_ref, posterior_ref):
     stride = 2 * own + 1
-    for d in range(devices):
-        lane = slice(d * LANES, (d + 1) * LANES)
-        evidence_ref[:, lane] = got_ref[d * stride : d * stride + own, :]
-        ess_ref[:, lane] = got_ref[d * stride + own : d * stride + 2 * own, :]
-    loglik = got_ref[pl.ds(2 * own, devices, stride=stride), :]
+    cols = devices * LANES
+    left = lax.broadcasted_iota(jnp.int32, (own, LANES), 1) < HALF
+    for g in range(devices // 2):
+        for k, ref in enumerate((evidence_ref, ess_ref)):
+            even = got_ref[2 * g * stride + k * own : 2 * g * stride + (k + 1) * own, :]
+            odd = got_ref[(2 * g + 1) * stride + k * own : (2 * g + 1) * stride + (k + 1) * own, :]
+            ref[:, g * LANES : (g + 1) * LANES] = jnp.where(left, even, swap(odd))
+            ref[:, cols // 2 + g * LANES : cols // 2 + (g + 1) * LANES] = jnp.where(left, swap(even), odd)
+    even = got_ref[pl.ds(2 * own, devices // 2, stride=2 * stride), :]
+    odd = got_ref[pl.ds(2 * own + stride, devices // 2, stride=2 * stride), :]
+    left = lax.broadcasted_iota(jnp.int32, (devices // 2, LANES), 1) < HALF
+    loglik = jnp.concatenate([jnp.where(left, even, swap(odd)), jnp.where(left, swap(even), odd)], axis=0)
     top = jnp.max(jnp.max(loglik, axis=0, keepdims=True), axis=1, keepdims=True)
     mass = jnp.exp(loglik - top)
     mass = jnp.sum(jnp.sum(mass, axis=0, keepdims=True), axis=1, keepdims=True)
@@ -352,6 +444,7 @@
         ),
         in_specs=[vmem],
         out_specs=(vmem, vmem, vmem),
+        compiler_params=pltpu.CompilerParams(vmem_limit_bytes=8 << 20),
     )(got)
 
 
@@ -361,12 +454,15 @@
     return got.reshape(x.shape)
 
 
-def column_body(devices, summary, kernel, grid_offset, log_prior, tile_event, tile_live):
-    tiles = tile_event.shape[0]
-    own = EVENTS // devices
-    sent = tile_stats(summary, kernel, grid_offset, log_prior, tile_event, tile_live)
-    merged = merge(exchange(sent, devices), devices, tiles)
-    evidence, ess, posterior = last(exchange(merged, devices), devices, own)
+def column_body(devices, *args):
+    tiles = args[4].shape[0]
+    sent = tile_stats(*args, 0)
+    got = exchange(sent, devices)
+    more = tile_stats(*args, 1)
+    rest = exchange(more, devices)
+    done, event = merge_first(got, devices, tiles)
+    merged = merge_second(rest, done, event, devices, tiles)
+    evidence, ess, posterior = last(exchange(merged, devices), devices, EVENTS // devices)
     return evidence, ess, posterior.reshape(-1)
 
 
@@ -422,9 +518,16 @@
     devices = mesh.shape["samp"]
 
     def body(summary, kernel, *rest):
-        tile_rows = summary.shape[0] // rest[2].shape[0]
-        whole_lanes = kernel.shape[1] == devices * LANES and tile_rows == LANES
-        if mesh.shape["grid"] == 1 and whole_lanes:
+        tiles, cols = rest[2].shape[0], kernel.shape[1]
+        fits = (
+            mesh.shape["grid"] == 1
+            and cols == devices * LANES
+            and cols % (4 * BLOCK) == 0
+            and summary.shape[0] == tiles * LANES
+            and tiles % 16 == 0
+            and EVENTS % devices == 0
+        )
+        if fits:
             return column_body(devices, summary, kernel, *rest)
         return row_body(summary, kernel, *rest)
 

time: 72.9 us -> 71.8 us (0.985)
  blocking collectives: 41.8 us -> 9.78 us
  starting transfers between devices: 0 us -> 15.7 us
  waiting for transfers between devices: 0 us -> 7.5 us
  Pallas kernels: 30.3 us -> 37.8 us
    all_to_all x2 -> x1, blocking collectives: 41.8 us -> 9.78 us  [exchange(): lax.all_to_all(x.reshape(devices, 1, width), 'samp', split_axis=0, concat...]
    all_to_all x0 -> x2, starting transfers between devices: none -> 15.7 us  [exchange(): lax.all_to_all(x.reshape(devices, 1, width), 'samp', split_axis=0, concat...]
    pallas_call x2 -> x4, Pallas kernels: 28.6 us -> 36.9 us  [the longest x2 30.9 us: tile_stats(): pl.pallas_call(functools.partial(stats_kernel, tiles, tile_rows, cols, pa...]
    all_to_all x0 -> x2, waiting for transfers between devices: none -> 7.5 us  [exchange(): lax.all_to_all(x.reshape(devices, 1, width), 'samp', split_axis=0, concat...]
    pallas_call x1, Pallas kernels: 1.68 us -> 0.87 us  [last(): pl.pallas_call(functools.partial(last_kernel, devices, own), out_shape=(j...]
  transfers between devices with their start and end apart: 0 -> 2, of which waited for: 0 -> 1; matrix products, arithmetic and copies ran while one was open for 0% -> 0% of each run, Pallas kernels for 0% -> 26%
where the time goes in v3:
time: 71.8 us; the launch traced here: 71.4 us
  Pallas kernels  37.8 us (53%)
  starting transfers between devices  15.7 us (22%)
  blocking collectives  9.78 us (14%)
  waiting for transfers between devices  7.5 us (10%)
    pallas_call x2, Pallas kernels, tile_stats(): pl.pallas_call(functools.partial(stats_kernel, tiles, tile_rows, cols, pa...  30.9 us
    all_to_all x2, starting transfers between devices, exchange(): lax.all_to_all(x.reshape(devices, 1, width), 'samp', split_axis=0, concat...  15.7 us
    all_to_all x1, blocking collectives, exchange(): lax.all_to_all(x.reshape(devices, 1, width), 'samp', split_axis=0, concat...  9.78 us
    all_to_all x2, waiting for transfers between devices, exchange(): lax.all_to_all(x.reshape(devices, 1, width), 'samp', split_axis=0, concat...  7.5 us
    pallas_call x1, Pallas kernels, merge_first(): pl.pallas_call(functools.partial(merge_first_kernel, devices, tiles), out...  3.07 us
    pallas_call x1, Pallas kernels, merge_second(): pl.pallas_call(functools.partial(merge_second_kernel, devices, tiles), ou...  2.97 us
  transfers between devices with their start and end apart: 2, of which 1 were waited for; matrix products, arithmetic and copies ran while one was open for 0% of the time, Pallas kernels for 26%

profile of v3, /device:TPU:0, one launch (start us, length us, event | category | flops | bytes accessed | tf_op | source)
XLA Modules:
  0.0 71.4 jit_solution(928618750657463636)
XLA Ops:
  0.6 15.4 %shard_map.86 = f32[544,128]{1,0:T(8,128)} custom-call(s32[16]{0:T(128)} %event_hbm.3, s32[16]{0:T(128)} %live_hbm.3, f32[1,4096]{1,0:T(1,128)} %bitcast.15, f32[16,128]{1,0:T(8,128)} %bitcast.18, bf16[2048,1024]{1,0:T(8,128)(2,1)} %summary_ref.3, bf16[1024,4096]{1,0:T(8,128)(2,1)} %kernel_ref.3), custom_call_target="tpu_custom_call" | custom-call | flops 4294967296 | bytes 8388608 | tf_op jit(solution)/shard_map/pallas_call | solution.py:236
  16.1 8.6 %all-to-all-start.1 = ((f32[32,1,2176]{2,1,0:T(1,128)}), f32[32,1,2176]{2,1,0:T(1,128)S(1)}, u32[]{:S(2)}, u32[]{:S(2)}) async-start(f32[32,1,2176]{2,1,0:T(1,128)} %bitcast.13), calls=%async_computation.1 | async-start | bytes 557056 | tf_op jit(solution)/shard_map/all_to_all | solution.py:453
  24.7 15.4 %shard_map.85 = f32[512,128]{1,0:T(8,128)} custom-call(s32[16]{0:T(128)} %event_hbm.3, s32[16]{0:T(128)} %live_hbm.3, f32[1,4096]{1,0:T(1,128)} %bitcast.16, f32[16,128]{1,0:T(8,128)} %bitcast.19, bf16[2048,1024]{1,0:T(8,128)(2,1)} %summary_ref.3, bf16[1024,4096]{1,0:T(8,128)(2,1)} %kernel_ref.3), custom_call_target="tpu_custom_call" | custom-call | flops 4294967296 | bytes 8388608 | tf_op jit(solution)/shard_map/pallas_call | solution.py:236
  40.1 0.0 all-to-all-done.1
  40.1 7.1 %all-to-all-start = ((f32[32,1,2048]{2,1,0:T(1,128)}), f32[32,1,2048]{2,1,0:T(1,128)S(1)}, u32[]{:S(2)}, u32[]{:S(2)}) async-start(f32[32,1,2048]{2,1,0:T(1,128)} %bitcast.14), calls=%async_computation | async-start | bytes 524288 | tf_op jit(solution)/shard_map/all_to_all | solution.py:453
  47.2 3.1 %shard_map.87 = (f32[192,128]{1,0:T(8,128)S(1)}, f32[512,128]{1,0:T(8,128)S(1)}) custom-call(f32[544,128]{1,0:T(8,128)S(1)} %bitcast.12), custom_call_target="tpu_custom_call" | custom-call | flops 400000000 | bytes 1000000 | tf_op jit(solution)/shard_map/pallas_call | solution.py:381
  50.3 7.5 %all-to-all-done = f32[32,1,2048]{2,1,0:T(1,128)S(1)} async-done(((f32[32,1,2048]{2,1,0:T(1,128)}), f32[32,1,2048]{2,1,0:T(1,128)S(1)}, u32[]{:S(2)}, u32[]{:S(2)}) %all-to-all-start) | async-done | bytes 262176 | tf_op jit(solution)/shard_map/all_to_all | solution.py:453
  57.8 3.0 %shard_map.88 = f32[160,128]{1,0:T(8,128)S(1)} custom-call(f32[512,128]{1,0:T(8,128)S(1)} %bitcast.9, f32[192,128]{1,0:T(8,128)S(1)} %get-tuple-element.8.done_ref, f32[512,128]{1,0:T(8,128)S(1)} %get-tuple-element.9.event_ref), custom_call_target="tpu_custom_call" | custom-call | tf_op jit(solution)/shard_map/pallas_call | solution.py:399
  60.8 9.8 %all_to_all.15 = f32[32,1,640]{2,1,0:T(1,128)S(1)} all-to-all(f32[32,1,640]{2,1,0:T(1,128)S(1)} %bitcast.11), channel_id=1, replica_groups=mesh['grid'=1,'samp'=32] {'samp'}, dimensions={0} | all-to-all | bytes 163840 | tf_op jit(solution)/shard_map/all_to_all | solution.py:453
  70.6 0.9 %shard_map.89 = (f32[2,4096]{1,0:T(2,128)}, f32[2,4096]{1,0:T(2,128)}, f32[32,128]{1,0:T(8,128)}) custom-call(f32[160,128]{1,0:T(8,128)S(1)} %bitcast.10), custom_call_target="tpu_custom_call" | custom-call | tf_op jit(solution)/shard_map/pallas_call | solution.py:438
Async XLA Ops:
  16.1 24.0 %all-to-all-start.1 = ((f32[32,1,2176]{2,1,0:T(1,128)}), f32[32,1,2176]{2,1,0:T(1,128)S(1)}, u32[]{:S(2)}, u32[]{:S(2)}) async-start(f32[32,1,2176]{2,1,0:T(1,128)} %bitcast.13), calls=%async_computation.1 | async-start | bytes 557056 | tf_op jit(solution)/shard_map/all_to_all | solution.py:453
  40.1 17.7 %all-to-all-start = ((f32[32,1,2048]{2,1,0:T(1,128)}), f32[32,1,2048]{2,1,0:T(1,128)S(1)}, u32[]{:S(2)}, u32[]{:S(2)}) async-start(f32[32,1,2048]{2,1,0:T(1,128)} %bitcast.14), calls=%async_computation | async-start | bytes 524288 | tf_op jit(solution)/shard_map/all_to_all | solution.py:453
